TPU v7x, 32 devices: a whole 2x2x4 slice. The times are simulated.
32 devices in a mesh: expert: 8 (over y, x, core), replica: 4 (over z).
Axes of the slice: x: 2, y: 2, z: 4, core: 2. Of those that a mesh axis runs over, the one named last changes fastest.
Arguments:
- tokens: bfloat16 [8192, 7168], P(('expert', 'replica')), may hold values from -40 to 40
- routes: int32 [8192, 8], P(('expert', 'replica')), may hold values from 0 to 255, all different within a row
- gate_weight: bfloat16 [7168, 4096], P(None, 'expert'), may hold values from -0.0625 to 0.0625
- up_weight: bfloat16 [7168, 4096], P(None, 'expert'), may hold values from -0.0625 to 0.0625
Outputs:
- calibrated: bfloat16 [512, 4096], P(('expert', 'replica'))
Inputs may be any that keep to these rules, and one draw needn't show every extreme that they name: `routes`: each row names 8 different experts of the layer, and every expert is named by some row.
All inputs are finite; a program needn't handle non-finite values.
Results may differ from a plain program's by a relative error of at most 0.001.
Values may be sent and summed in bfloat16 or wider, within the bound.
A program may use at most 128 MiB of HBM per device.

v0:
```python
import math
import jax
import jax.numpy as jnp
from jax import lax
from jax.sharding import PartitionSpec as P

D = 7168
HSPLIT = 4
CAP = 16
KMOM = 12
QITERS = 4
QUANTILE_LEVEL = 0.99
EPSILON = 1e-06


def build_slots(routes, experts):
    window = jnp.arange(experts, dtype=jnp.int32)
    naming = jnp.sum((routes[:, :, None] == window[None, None, :]).astype(jnp.int32), axis=1)
    before = jnp.cumsum(naming, axis=0) - naming
    positions = jnp.arange(CAP, dtype=jnp.int32)
    chosen = naming[:, :, None] * (before[:, :, None] == positions[None, None, :]).astype(jnp.int32)
    token_ids = jnp.arange(routes.shape[0], dtype=jnp.int32)
    picked = jnp.sum(chosen * token_ids[:, None, None], axis=0)
    filled = jnp.sum(chosen, axis=0)
    return (picked, filled)


def chebyshev_sums(scaled, occupied):
    previous = jnp.ones_like(scaled)
    current = scaled
    totals = [
        jnp.sum(occupied[:, None] * previous, axis=0),
        jnp.sum(occupied[:, None] * current, axis=0),
    ]
    for degree in range(2, KMOM):
        previous, current = (current, 2.0 * scaled * current - previous)
        totals.append(jnp.sum(occupied[:, None] * current, axis=0))
    return jnp.stack(totals[:KMOM])


def clip_fraction(moments, counted):
    coefficient = moments[1:] / counted[None, :]
    orders = jnp.arange(1, KMOM, dtype=jnp.float32)[:, None]
    angles = jnp.full(moments.shape[1:], 0.5 * math.pi, jnp.float32)
    for iteration in range(QITERS):
        lower_mass = (
            1.0
            - angles / math.pi
            - 2.0
            / math.pi
            * jnp.sum(coefficient * jnp.sin(orders * angles[None, :]) / orders, axis=0)
        )
        angles = angles + math.pi * (lower_mass - QUANTILE_LEVEL)
    return 0.5 * (1.0 + jnp.cos(angles))


def shards(tokens, routes, gate_weight, up_weight):
    devices_e = lax.axis_size("expert")
    experts = devices_e // HSPLIT
    shard_width = gate_weight.shape[1]
    picked, filled = build_slots(routes, experts)
    occupied = filled.astype(jnp.bfloat16)
    gathered = jnp.take(tokens, picked.reshape(-1), axis=0).reshape(experts, CAP, D)
    gathered = gathered * occupied[:, :, None]
    outgoing = jnp.repeat(gathered, HSPLIT, axis=0)
    presence = jnp.repeat(occupied, HSPLIT, axis=0)
    received = lax.all_to_all(outgoing, "expert", split_axis=0, concat_axis=0, tiled=True)
    flat_rows = received.reshape(-1, D)
    gate_act = jnp.dot(flat_rows, gate_weight, preferred_element_type=jnp.float32)
    up_act = jnp.dot(flat_rows, up_weight, preferred_element_type=jnp.float32)
    hidden = jax.nn.silu(gate_act) * up_act
    hidden, present = (
        hidden.reshape(received.shape[:-1] + (shard_width,)),
        lax.all_to_all(presence, "expert", split_axis=0, concat_axis=0, tiled=True),
    )
    magnitude = jnp.abs(hidden)
    ceiling = lax.pmax(jnp.max(magnitude, axis=(0, 1)), "replica") + EPSILON
    scaled = 2.0 * magnitude / ceiling - 1.0
    local_sums = chebyshev_sums(
        scaled.reshape(-1, shard_width), present.reshape(-1).astype(jnp.float32)
    )
    moments = lax.psum(local_sums, "replica")
    clip_level = ceiling * clip_fraction(moments, moments[0])
    calibrated = (jnp.clip(hidden, -clip_level, clip_level) / ceiling).astype(jnp.bfloat16)
    returned = lax.all_to_all(calibrated, "expert", split_axis=0, concat_axis=2, tiled=True)
    return returned.reshape(CAP, experts * HSPLIT * shard_width)


def solution(mesh):
    in_specs = (
        P(("expert", "replica"), None),
        P(("expert", "replica"), None),
        P(None, "expert"),
        P(None, "expert"),
    )
    out_specs = P(("expert", "replica"), None)
    return jax.shard_map(shards, mesh=mesh, in_specs=in_specs, out_specs=out_specs, check_vma=False)
```

profile of v0, /device:TPU:0, one launch (start us, length us, event | category | flops | bytes accessed | tf_op | source)
XLA Modules:
  0.0 88.1 jit_solution(15963084966948955778)
XLA Ops:
  0.0 0.7 convert_reduce_fusion
  0.7 0.6 reduce-window.6
  1.3 0.2 slice_reduce_fusion
  1.6 0.2 reduce-window.9
  1.7 0.1 add_bitcast_fusion
  1.8 0.2 select_reduce_fusion
  2.0 0.6 copy.18
  2.6 5.2 %all-to-all-start.1 = ((bf16[8,1,16]{2,1,0:T(2,128)(2,1)}), bf16[8,1,16]{2,1,0:T(2,128)(2,1)S(1)}, u32[]{:S(2)}, u32[]{:S(2)}) async-start(bf16[8,1,16]{2,1,0:T(2,128)(2,1)} %copy.18), calls=%async_computation.1 | async-start | bytes 8192 | tf_op jit(solution)/shard_map/all_to_all | solution.py:74
  7.8 0.1 reshape.125
  7.9 3.8 %gather_fusion = bf16[32,7168]{1,0:T(8,128)(2,1)S(1)} fusion(bf16[256,7168]{1,0:T(8,128)(2,1)} %param.4, s32[1024]{0:T(1024)S(1)} %pad_clamp_fusion), kind=kCustom, calls=%fused_computation | custom fusion | bytes 917632 | tf_op jit(solution)/shard_map/jit(_take)/gather | solution.py:63
  11.7 0.1 select_multiply_fusion
  11.8 0.6 all-to-all-done.1
  12.4 1.4 %broadcast_in_dim.20 = bf16[2,4,16,7168]{3,2,1,0:T(8,128)(2,1)} broadcast(bf16[2,16,7168]{2,1,0:T(8,128)(2,1)S(1)} %select_multiply_fusion), dimensions={0,2,3} | broadcast | bytes 2293760 | tf_op jit(solution)/shard_map/broadcast_in_dim | solution.py:65
  13.8 3.6 %all-to-all-start = ((bf16[8,16,7168]{2,1,0:T(8,128)(2,1)}), bf16[8,16,7168]{2,1,0:T(8,128)(2,1)S(1)}, u32[]{:S(2)}, u32[]{:S(2)}) async-start(bf16[8,16,7168]{2,1,0:T(8,128)(2,1)} %bitcast.45), calls=%async_computation | async-start | bytes 3670016 | tf_op jit(solution)/shard_map/all_to_all | solution.py:67
  17.5 0.6 convert_reduce_fusion.1
  18.1 0.1 reshape.130
  18.2 23.0 %all-to-all-done = bf16[8,16,7168]{2,1,0:T(8,128)(2,1)S(1)} async-done(((bf16[8,16,7168]{2,1,0:T(8,128)(2,1)}), bf16[8,16,7168]{2,1,0:T(8,128)(2,1)S(1)}, u32[]{:S(2)}, u32[]{:S(2)}) %all-to-all-start) | async-done | bytes 1835040 | tf_op jit(solution)/shard_map/all_to_all | solution.py:67
  41.2 4.2 %fusion.8 = f32[128,512]{1,0:T(8,128)S(1)} fusion(bf16[128,7168]{1,0:T(8,128)(2,1)S(1)} %bitcast.43, bf16[7168,512]{1,0:T(8,128)(2,1)} %param.6), kind=kOutput, calls=%fused_computation.60 | convolution fusion | flops 939524096 | bytes 9437184 | tf_op jit(solution)/shard_map/dot_general | solution.py:69
  45.5 4.2 %abs_reduce_fusion = (f32[512]{0:T(512)S(1)}, f32[128,512]{1,0:T(8,128)S(1)}) fusion(bf16[128,7168]{1,0:T(8,128)(2,1)S(1)} %bitcast.44, bf16[7168,512]{1,0:T(8,128)(2,1)} %param.7, f32[128,512]{1,0:T(8,128)S(1)} %fusion.8), kind=kOutput, calls=%fused_computation.25 | convolution fusion | flops 939982336 | bytes 9701376 | tf_op jit(solution)/shard_map/dot_general | solution.py:70
  49.7 12.0 %pmax.7 = f32[512]{0:T(512)S(1)} all-reduce(f32[512]{0:T(512)S(1)} %get-tuple-element.22), channel_id=1, replica_groups=mesh['expert'=8,'replica'=4] {'replica'}, use_global_device_ids=true, to_apply=%region_6.7 | all-reduce | flops 512 | bytes 4096 | tf_op jit(solution)/shard_map/pmax | solution.py:77
  61.7 0.5 multiply_reduce_fusion
  62.1 0.6 stack.39
  62.8 0.1 stack.51
  62.9 15.8 %psum.7 = f32[12,512]{1,0:T(8,128)S(1)} all-reduce(f32[12,512]{1,0:T(8,128)S(1)} %stack.51), channel_id=1, replica_groups=mesh['expert'=8,'replica'=4] {'replica'}, use_global_device_ids=true, to_apply=%region_19.20 | all-reduce | flops 6144 | bytes 49152 | tf_op jit(solution)/shard_map/psum | solution.py:82
  78.7 0.1 fusion.1
  78.8 0.2 fusion.2
  79.0 0.2 fusion.3
  79.2 0.2 fusion.4
  79.5 0.1 fusion.7
  79.6 7.9 %all_to_all.29 = bf16[8,16,512]{2,1,0:T(8,128)(2,1)S(1)} all-to-all(bf16[8,16,512]{2,1,0:T(8,128)(2,1)S(1)} %divide_convert_fusion), channel_id=1, replica_groups=mesh['expert'=8,'replica'=4] {'expert'}, dimensions={0} | all-to-all | bytes 262144 | tf_op jit(solution)/shard_map/all_to_all | solution.py:85
  87.5 0.7 copy.21
  (15 shorter events, 0.2 us)
Async XLA Ops:
  2.6 9.8 %all-to-all-start.1 = ((bf16[8,1,16]{2,1,0:T(2,128)(2,1)}), bf16[8,1,16]{2,1,0:T(2,128)(2,1)S(1)}, u32[]{:S(2)}, u32[]{:S(2)}) async-start(bf16[8,1,16]{2,1,0:T(2,128)(2,1)} %copy.18), calls=%async_computation.1 | async-start | bytes 8192 | tf_op jit(solution)/shard_map/all_to_all | solution.py:74
  13.8 27.4 %all-to-all-start = ((bf16[8,16,7168]{2,1,0:T(8,128)(2,1)}), bf16[8,16,7168]{2,1,0:T(8,128)(2,1)S(1)}, u32[]{:S(2)}, u32[]{:S(2)}) async-start(bf16[8,16,7168]{2,1,0:T(8,128)(2,1)} %bitcast.45), calls=%async_computation | async-start | bytes 3670016 | tf_op jit(solution)/shard_map/all_to_all | solution.py:67
where the time goes:
time: 88.6 us; the launch traced here: 88.1 us
  blocking collectives  35.6 us (40%)
  waiting for transfers between devices  23.7 us (27%)
  starting transfers between devices  8.79 us (10%)
  matrix products  8.45 us (10%)
  local copies, waits for them, and re-layouts  7.57 us (9%)
  other arithmetic  3.88 us (4%)
    all_to_all x1, waiting for transfers between devices, shards(): lax.all_to_all(outgoing, 'expert', split_axis=0, concat_axis=0, tiled=True)  23 us
    psum x1, blocking collectives, shards(): moments = lax.psum(local_sums, 'replica')  15.8 us
    pmax x1, blocking collectives, shards(): ceiling = lax.pmax(jnp.max(magnitude, axis=(0, 1)), 'replica') + EPSILON  12 us
    all_to_all x1, blocking collectives, shards(): lax.all_to_all(calibrated, 'expert', split_axis=0, concat_axis=2, tiled=T...  7.89 us
    all_to_all x1, starting transfers between devices, shards(): lax.all_to_all(presence, 'expert', split_axis=0, concat_axis=0, tiled=True)  5.2 us
    dot_general x1, matrix products, shards(): up_act = jnp.dot(flat_rows, up_weight, preferred_element_type=jnp.float32)  4.23 us
    dot_general x1, matrix products, shards(): jnp.dot(flat_rows, gate_weight, preferred_element_type=jnp.float32)  4.22 us
    gather x1, local copies, waits for them, and re-layouts, shards(): jnp.take(tokens, picked.reshape(-1), axis=0).reshape(experts, CAP, D)  3.76 us
  transfers between devices with their start and end apart: 2, of which 2 were waited for; matrix products, arithmetic and copies ran while one was open for 5% of the time, Pallas kernels for 0%

commit v1 on v0

--- a/solution.py
+++ b/solution.py
@@ -79,7 +79,9 @@
     local_sums = chebyshev_sums(
         scaled.reshape(-1, shard_width), present.reshape(-1).astype(jnp.float32)
     )
-    moments = lax.psum(local_sums, "replica")
+    moments = local_sums
+    for hop in (1, 2):
+        moments = moments + lax.ppermute(moments, "replica", [(dev, dev ^ hop) for dev in range(4)])
     clip_level = ceiling * clip_fraction(moments, moments[0])
     calibrated = (jnp.clip(hidden, -clip_level, clip_level) / ceiling).astype(jnp.bfloat16)
     returned = lax.all_to_all(calibrated, "expert", split_axis=0, concat_axis=2, tiled=True)

time: 88.6 us -> 81.6 us (0.921)
  blocking collectives: 35.6 us -> 19.9 us
  waiting for transfers between devices: 23.7 us -> 32.4 us
    psum x1 -> x0, blocking collectives: 15.8 us -> none  [shards(): moments = lax.psum(local_sums, 'replica')]
    ppermute x0 -> x2, waiting for transfers between devices: none -> 8.65 us  [shards(): lax.ppermute(moments, 'replica', [(dev, dev ^ hop) for dev in range(4)])]
  transfers between devices with their start and end apart: 2 -> 4, of which waited for: 2 -> 4; matrix products, arithmetic and copies ran while one was open for 5% -> 6% of each run, Pallas kernels for 0% -> 0%
where the time goes in v1:
time: 81.6 us; the launch traced here: 81.1 us
  waiting for transfers between devices  32.4 us (40%)
  blocking collectives  19.9 us (24%)
  starting transfers between devices  8.86 us (11%)
  matrix products  8.45 us (10%)
  local copies, waits for them, and re-layouts  7.57 us (9%)
  other arithmetic  3.9 us (5%)
    all_to_all x1, waiting for transfers between devices, shards(): lax.all_to_all(outgoing, 'expert', split_axis=0, concat_axis=0, tiled=True)  23.1 us
    pmax x1, blocking collectives, shards(): ceiling = lax.pmax(jnp.max(magnitude, axis=(0, 1)), 'replica') + EPSILON  12 us
    ppermute x2, waiting for transfers between devices, shards(): lax.ppermute(moments, 'replica', [(dev, dev ^ hop) for dev in range(4)])  8.65 us
    all_to_all x1, blocking collectives, shards(): lax.all_to_all(calibrated, 'expert', split_axis=0, concat_axis=2, tiled=T...  7.89 us
    all_to_all x1, starting transfers between devices, shards(): lax.all_to_all(presence, 'expert', split_axis=0, concat_axis=0, tiled=True)  5.2 us
    dot_general x1, matrix products, shards(): up_act = jnp.dot(flat_rows, up_weight, preferred_element_type=jnp.float32)  4.23 us
    dot_general x1, matrix products, shards(): jnp.dot(flat_rows, gate_weight, preferred_element_type=jnp.float32)  4.22 us
    gather x1, local copies, waits for them, and re-layouts, shards(): jnp.take(tokens, picked.reshape(-1), axis=0).reshape(experts, CAP, D)  3.76 us
  transfers between devices with their start and end apart: 4, of which 4 were waited for; matrix products, arithmetic and copies ran while one was open for 6% of the time, Pallas kernels for 0%

profile of v1, /device:TPU:0, one launch (start us, length us, event | category | flops | bytes accessed | tf_op | source)
XLA Modules:
  0.0 81.1 jit_solution(14671711066721324593)
XLA Ops:
  0.0 0.7 convert_reduce_fusion
  0.7 0.6 reduce-window.6
  1.3 0.2 slice_reduce_fusion
  1.6 0.2 reduce-window.9
  1.7 0.1 add_bitcast_fusion
  1.8 0.2 select_reduce_fusion
  2.0 0.6 copy.18
  2.6 5.2 %all-to-all-start.1 = ((bf16[8,1,16]{2,1,0:T(2,128)(2,1)}), bf16[8,1,16]{2,1,0:T(2,128)(2,1)S(1)}, u32[]{:S(2)}, u32[]{:S(2)}) async-start(bf16[8,1,16]{2,1,0:T(2,128)(2,1)} %copy.18), calls=%async_computation.1 | async-start | bytes 8192 | tf_op jit(solution)/shard_map/all_to_all | solution.py:74
  7.8 0.1 reshape.125
  7.9 3.8 %gather_fusion = bf16[32,7168]{1,0:T(8,128)(2,1)S(1)} fusion(bf16[256,7168]{1,0:T(8,128)(2,1)} %param.4, s32[1024]{0:T(1024)S(1)} %pad_clamp_fusion), kind=kCustom, calls=%fused_computation | custom fusion | bytes 917632 | tf_op jit(solution)/shard_map/jit(_take)/gather | solution.py:63
  11.7 0.1 select_multiply_fusion
  11.8 0.6 all-to-all-done.1
  12.4 1.4 %broadcast_in_dim.20 = bf16[2,4,16,7168]{3,2,1,0:T(8,128)(2,1)} broadcast(bf16[2,16,7168]{2,1,0:T(8,128)(2,1)S(1)} %select_multiply_fusion), dimensions={0,2,3} | broadcast | bytes 2293760 | tf_op jit(solution)/shard_map/broadcast_in_dim | solution.py:65
  13.8 3.6 %all-to-all-start = ((bf16[8,16,7168]{2,1,0:T(8,128)(2,1)}), bf16[8,16,7168]{2,1,0:T(8,128)(2,1)S(1)}, u32[]{:S(2)}, u32[]{:S(2)}) async-start(bf16[8,16,7168]{2,1,0:T(8,128)(2,1)} %bitcast.45), calls=%async_computation | async-start | bytes 3670016 | tf_op jit(solution)/shard_map/all_to_all | solution.py:67
  17.4 0.6 convert_reduce_fusion.1
  18.1 0.1 reshape.130
  18.1 23.1 %all-to-all-done = bf16[8,16,7168]{2,1,0:T(8,128)(2,1)S(1)} async-done(((bf16[8,16,7168]{2,1,0:T(8,128)(2,1)}), bf16[8,16,7168]{2,1,0:T(8,128)(2,1)S(1)}, u32[]{:S(2)}, u32[]{:S(2)}) %all-to-all-start) | async-done | bytes 1835040 | tf_op jit(solution)/shard_map/all_to_all | solution.py:67
  41.2 4.2 %fusion.8 = f32[128,512]{1,0:T(8,128)S(1)} fusion(bf16[128,7168]{1,0:T(8,128)(2,1)S(1)} %bitcast.43, bf16[7168,512]{1,0:T(8,128)(2,1)} %param.6), kind=kOutput, calls=%fused_computation.60 | convolution fusion | flops 939524096 | bytes 9437184 | tf_op jit(solution)/shard_map/dot_general | solution.py:69
  45.5 4.2 %abs_reduce_fusion = (f32[512]{0:T(512)S(1)}, f32[128,512]{1,0:T(8,128)S(1)}) fusion(bf16[128,7168]{1,0:T(8,128)(2,1)S(1)} %bitcast.44, bf16[7168,512]{1,0:T(8,128)(2,1)} %param.7, f32[128,512]{1,0:T(8,128)S(1)} %fusion.8), kind=kOutput, calls=%fused_computation.25 | convolution fusion | flops 939982336 | bytes 9701376 | tf_op jit(solution)/shard_map/dot_general | solution.py:70
  49.7 12.0 %pmax.7 = f32[512]{0:T(512)S(1)} all-reduce(f32[512]{0:T(512)S(1)} %get-tuple-element.22), channel_id=1, replica_groups=mesh['expert'=8,'replica'=4] {'replica'}, use_global_device_ids=true, to_apply=%region_6.7 | all-reduce | flops 512 | bytes 4096 | tf_op jit(solution)/shard_map/pmax | solution.py:77
  61.7 0.5 multiply_reduce_fusion
  62.1 0.6 stack.39
  62.8 0.1 stack.51
  62.9 0.1 collective-permute-start
  63.0 3.9 %collective-permute-done = f32[12,512]{1,0:T(8,128)S(1)} collective-permute-done((f32[12,512]{1,0:T(8,128)S(1)}, f32[12,512]{1,0:T(8,128)S(1)}, u32[]{:S(2)}, u32[]{:S(2)}) %collective-permute-start) | collective-permute-done | bytes 24608 | tf_op jit(solution)/shard_map/ppermute | solution.py:84
  66.9 0.0 collective-permute-start.1
  66.9 4.8 %collective-permute-done.1 = f32[12,512]{1,0:T(8,128)S(1)} collective-permute-done((f32[12,512]{1,0:T(8,128)S(1)}, f32[12,512]{1,0:T(8,128)S(1)}, u32[]{:S(2)}, u32[]{:S(2)}) %collective-permute-start.1) | collective-permute-done | bytes 24608 | tf_op jit(solution)/shard_map/ppermute | solution.py:84
  71.7 0.1 fusion.1
  71.8 0.2 fusion.2
  72.0 0.2 fusion.3
  72.3 0.2 fusion.4
  72.5 0.1 fusion.7
  72.6 7.9 %all_to_all.29 = bf16[8,16,512]{2,1,0:T(8,128)(2,1)S(1)} all-to-all(bf16[8,16,512]{2,1,0:T(8,128)(2,1)S(1)} %divide_convert_fusion), channel_id=1, replica_groups=mesh['expert'=8,'replica'=4] {'expert'}, dimensions={0} | all-to-all | bytes 262144 | tf_op jit(solution)/shard_map/all_to_all | solution.py:87
  80.5 0.7 copy.21
  (17 shorter events, 0.2 us)
Async XLA Ops:
  2.6 9.8 %all-to-all-start.1 = ((bf16[8,1,16]{2,1,0:T(2,128)(2,1)}), bf16[8,1,16]{2,1,0:T(2,128)(2,1)S(1)}, u32[]{:S(2)}, u32[]{:S(2)}) async-start(bf16[8,1,16]{2,1,0:T(2,128)(2,1)} %copy.18), calls=%async_computation.1 | async-start | bytes 8192 | tf_op jit(solution)/shard_map/all_to_all | solution.py:74
  13.8 27.4 %all-to-all-start = ((bf16[8,16,7168]{2,1,0:T(8,128)(2,1)}), bf16[8,16,7168]{2,1,0:T(8,128)(2,1)S(1)}, u32[]{:S(2)}, u32[]{:S(2)}) async-start(bf16[8,16,7168]{2,1,0:T(8,128)(2,1)} %bitcast.45), calls=%async_computation | async-start | bytes 3670016 | tf_op jit(solution)/shard_map/all_to_all | solution.py:67
  62.9 4.0 %collective-permute-start = (f32[12,512]{1,0:T(8,128)S(1)}, f32[12,512]{1,0:T(8,128)S(1)}, u32[]{:S(2)}, u32[]{:S(2)}) collective-permute-start(f32[12,512]{1,0:T(8,128)S(1)} %stack.51), channel_id=1, source_target_pairs={{0,1},{1,0},{2,3},{3,2},{4,5},{5,4},{6,7},{7,6},{8,9},{9,8},{10,11... | collective-permute-start | bytes 73736 | tf_op jit(solution)/shard_map/ppermute | solution.py:84
  66.9 4.8 %collective-permute-start.1 = (f32[12,512]{1,0:T(8,128)S(1)}, f32[12,512]{1,0:T(8,128)S(1)}, u32[]{:S(2)}, u32[]{:S(2)}) collective-permute-start(f32[12,512]{1,0:T(8,128)S(1)} %add.112), channel_id=1, source_target_pairs={{0,2},{1,3},{2,0},{3,1},{4,6},{5,7},{6,4},{7,5},{8,10},{9,11},{10,... | collective-permute-start | bytes 73736 | tf_op jit(solution)/shard_map/ppermute | solution.py:84
